TPU v7x, 256 devices: a whole 4x4x8 slice. The times are simulated.
256 devices in a mesh: blk: 8 (over x, y_hi), tile: 32 (over z, y_lo, core).
Axes of the slice: x: 4, y: 4 (y_hi: 2, y_lo: 2; y = y_hi * 2 + y_lo), z: 8, core: 2. Of those that a mesh axis runs over, the one named last changes fastest.
Arguments:
- grid_feat: bfloat16 [65536, 512], P(('blk', 'tile')), may hold values from -18 to 18
- queries: bfloat16 [65536, 512], P(('blk', 'tile')), may hold values from -90 to 90
- obs_keys: bfloat16 [2048, 512], P(('blk', 'tile')), may hold values from -4 to 4
- obs_values: bfloat16 [2048, 512], P(('blk', 'tile')), may hold values from -6 to 6
- block_mask: int32 [512, 16], P(('blk', 'tile')), may hold values from 0 to 1, as said below
- obs_valid: int32 [16], replicated, may hold values from 2 to 128, as said below
- out_weight: bfloat16 [512, 512], replicated, may hold values from -0.25 to 0.25
- conv_weight: bfloat16 [3, 3, 512, 512], replicated, may hold values from -0.09375 to 0.09375
Outputs:
- layer_out: bfloat16 [65536, 512], P(('blk', 'tile'))
Inputs may be any that keep to these rules, and one draw needn't show every extreme that they name: `block_mask`: row t has a 1 in column t mod 16. `obs_valid`: at least one entry equals 128.
All inputs are finite; a program needn't handle non-finite values.
Results may differ from a plain program's by a relative error of at most 0.007.
Values may be sent and summed in bfloat16 or wider, within the bound.
A program may use at most 64 MiB of HBM per device.

v0:
```python
import jax
import jax.numpy as jnp
from jax import lax
from jax.sharding import PartitionSpec as P

HEADS = 8
OBS_BLOCK = 128


def passed_along(array, axis, by):
    peers = lax.axis_size(axis)
    return lax.ppermute(array, axis, [(i, (i + by) % peers) for i in range(peers)])


def with_halo(block, sides, width):
    for axis, dim in sides:
        count = lax.axis_size(axis)
        forward = [(i, i + 1) for i in range(count - 1)]
        backward = [(target, source) for source, target in forward]
        low = lax.ppermute(
            lax.slice_in_dim(block, block.shape[dim] - width, None, axis=dim), axis, forward
        )
        high = lax.ppermute(lax.slice_in_dim(block, 0, width, axis=dim), axis, backward)
        block = jnp.concatenate([low, block, high], axis=dim)
    return block


def circulate(block, visit, carry):
    home = lax.axis_index("blk")
    count = lax.axis_size("blk")
    carry = visit(carry, block, home)
    for step in range(1, count):
        block = passed_along(block, "blk", 1)
        carry = visit(carry, block, (home - step) % count)
    return carry


def on_device(
    grid_feat, queries, obs_keys, obs_values, block_mask, obs_valid, out_weight, conv_weight
):
    q_dev, width = queries.shape
    head = width // HEADS
    scale = head ** (-0.5)
    tiles = block_mask.shape[0]
    nblocks = block_mask.shape[1]
    lon = q_dev // tiles
    group_rows = obs_keys.shape[0] * lax.axis_size("tile")
    query_heads = queries.reshape(q_dev, HEADS, head)
    mask_float = block_mask.astype(jnp.float32)
    block_ids = jnp.arange(nblocks, dtype=jnp.int32)

    def attend(carry, kv_rows, start):
        rows = kv_rows.shape[1]
        key_index = start + jnp.arange(rows, dtype=jnp.int32)
        member = (key_index // OBS_BLOCK)[:, None] == block_ids[None, :]
        limits = jnp.sum(jnp.where(member, obs_valid[None, :], 0), axis=1)
        live = key_index % OBS_BLOCK < limits
        wanted = (
            jnp.dot(mask_float, member.astype(jnp.float32).T, precision=lax.Precision.HIGHEST) > 0.5
        )
        allowed = wanted & live[None, :]
        top, total, acc = carry
        keys = kv_rows[0].reshape(rows, HEADS, head)
        values = kv_rows[1].reshape(rows, HEADS, head)
        scores = (
            jnp.einsum("qhd,khd->hqk", query_heads, keys, preferred_element_type=jnp.float32)
            * scale
        )
        scores = scores.reshape(HEADS, tiles, lon, rows)
        scores = jnp.where(allowed[None, :, None, :], scores, -jnp.inf).reshape(HEADS, q_dev, rows)
        new_top = jnp.maximum(top, jnp.max(scores, axis=-1))
        factor = jnp.exp(top - new_top)
        weights = jnp.exp(scores - new_top[..., None])
        total = total * factor + jnp.sum(weights, axis=-1)
        acc = acc * factor[..., None] + jnp.einsum(
            "hqk,khd->hqd", weights.astype(jnp.bfloat16), values, preferred_element_type=jnp.float32
        )
        return (new_top, total, acc)

    start_state = (
        jnp.full((HEADS, q_dev), -1e30, jnp.float32),
        jnp.zeros((HEADS, q_dev), jnp.float32),
        jnp.zeros((HEADS, q_dev, head), jnp.float32),
    )
    kv_local = jnp.stack([obs_keys, obs_values])

    def visit_shards(carry, block, owner):
        collected = lax.all_gather(block, "tile", axis=1, tiled=True)
        return attend(carry, collected, owner * group_rows)

    state = circulate(kv_local, visit_shards, start_state)
    top, total, acc = state
    mixed = (
        jnp.transpose(acc / total[..., None], (1, 0, 2)).reshape(q_dev, width).astype(jnp.bfloat16)
    )
    projected = jnp.dot(mixed, out_weight, preferred_element_type=jnp.float32)
    hidden = lax.optimization_barrier(
        (grid_feat.astype(jnp.float32) + projected).astype(jnp.bfloat16)
    )
    wide = hidden.astype(jnp.float32)
    normed = (wide * lax.rsqrt(jnp.mean(wide * wide, axis=-1, keepdims=True) + 1e-06)).astype(
        jnp.bfloat16
    )
    field = normed.reshape(tiles, lon, width)
    padded = with_halo(field, ((("blk", "tile"), 0),), 1)
    summed = jnp.zeros((q_dev, width), jnp.float32)
    for lat_off in range(3):
        for lon_off in range(3):
            moved = jnp.roll(padded[lat_off : lat_off + tiles], 1 - lon_off, axis=1)
            summed = summed + jnp.dot(
                moved.reshape(q_dev, width),
                conv_weight[lat_off, lon_off],
                preferred_element_type=jnp.float32,
            )
    return (wide + summed).astype(jnp.bfloat16)


def solution(mesh):
    in_specs = (
        P(("blk", "tile"), None),
        P(("blk", "tile"), None),
        P(("blk", "tile"), None),
        P(("blk", "tile"), None),
        P(("blk", "tile"), None),
        P(),
        P(),
        P(),
    )
    out_specs = P(("blk", "tile"), None)
    return jax.shard_map(
        on_device, mesh=mesh, in_specs=in_specs, out_specs=out_specs, check_vma=False
    )
```

profile of v0, /device:TPU:2, one launch (start us, length us, event | category | flops | bytes accessed | tf_op | source)
XLA Modules:
  0.0 370.2 jit_solution(6822890569749922319)
XLA Ops:
  1.4 3.2 collective-permute-start
  4.6 38.0 %all_gather.24 = bf16[2,256,512]{2,1,0:T(8,128)(2,1)S(1)} all-gather(bf16[2,8,512]{2,1,0:T(8,128)(2,1)} %pad_maximum_fusion.6), channel_id=1, replica_groups=mesh['blk'=8,'tile'=32] {'tile'}, dimensions={1}, use_global_device_ids=true | all-gather | bytes 540672 | tf_op jit(solution)/shard_map/all_gather | solution.py:88
  58.9 32.3 %all_gather.25 = bf16[2,256,512]{2,1,0:T(8,128)(2,1)S(1)} all-gather(bf16[2,8,512]{2,1,0:T(8,128)(2,1)} %collective-permute-done), channel_id=1, replica_groups=mesh['blk'=8,'tile'=32] {'tile'}, dimensions={1}, use_global_device_ids=true | all-gather | bytes 540672 | tf_op jit(solution)/shard_map/all_gather | solution.py:88
  92.2 2.8 collective-permute-start.1
  95.0 2.8 fusion.161
  99.2 33.5 %all_gather.26 = bf16[2,256,512]{2,1,0:T(8,128)(2,1)S(1)} all-gather(bf16[2,8,512]{2,1,0:T(8,128)(2,1)S(1)} %collective-permute-done.1), channel_id=1, replica_groups=mesh['blk'=8,'tile'=32] {'tile'}, dimensions={1}, use_global_device_ids=true | all-gather | bytes 540672 | tf_op jit(solution)/shard_map/all_gather | solution.py:88
  133.5 2.4 collective-permute-start.2
  135.9 3.4 fusion.160
  140.7 31.9 %all_gather.27 = bf16[2,256,512]{2,1,0:T(8,128)(2,1)S(1)} all-gather(bf16[2,8,512]{2,1,0:T(8,128)(2,1)S(1)} %collective-permute-done.2), channel_id=1, replica_groups=mesh['blk'=8,'tile'=32] {'tile'}, dimensions={1}, use_global_device_ids=true | all-gather | bytes 540672 | tf_op jit(solution)/shard_map/all_gather | solution.py:88
  173.6 2.7 collective-permute-start.3
  176.3 3.4 fusion.159
  181.1 33.0 %all_gather.28 = bf16[2,256,512]{2,1,0:T(8,128)(2,1)S(1)} all-gather(bf16[2,8,512]{2,1,0:T(8,128)(2,1)S(1)} %collective-permute-done.3), channel_id=1, replica_groups=mesh['blk'=8,'tile'=32] {'tile'}, dimensions={1}, use_global_device_ids=true | all-gather | bytes 540672 | tf_op jit(solution)/shard_map/all_gather | solution.py:88
  215.0 2.8 fusion.158
  217.9 2.9 collective-permute-start.4
  222.2 1.8 collective-permute-done.4
  224.6 32.5 %all_gather.29 = bf16[2,256,512]{2,1,0:T(8,128)(2,1)S(1)} all-gather(bf16[2,8,512]{2,1,0:T(8,128)(2,1)S(1)} %collective-permute-done.4), channel_id=1, replica_groups=mesh['blk'=8,'tile'=32] {'tile'}, dimensions={1}, use_global_device_ids=true | all-gather | bytes 540672 | tf_op jit(solution)/shard_map/all_gather | solution.py:88
  259.3 3.5 fusion.157
  265.0 33.1 %all_gather.30 = bf16[2,256,512]{2,1,0:T(8,128)(2,1)S(1)} all-gather(bf16[2,8,512]{2,1,0:T(8,128)(2,1)S(1)} %collective-permute-done.5), channel_id=1, replica_groups=mesh['blk'=8,'tile'=32] {'tile'}, dimensions={1}, use_global_device_ids=true | all-gather | bytes 540672 | tf_op jit(solution)/shard_map/all_gather | solution.py:88
  298.9 2.9 collective-permute-start.6
  301.8 3.4 fusion.156
  306.0 31.8 %all_gather.31 = bf16[2,256,512]{2,1,0:T(8,128)(2,1)S(1)} all-gather(bf16[2,8,512]{2,1,0:T(8,128)(2,1)S(1)} %collective-permute-done.6), channel_id=1, replica_groups=mesh['blk'=8,'tile'=32] {'tile'}, dimensions={1}, use_global_device_ids=true | all-gather | bytes 540672 | tf_op jit(solution)/shard_map/all_gather | solution.py:88
  353.9 2.3 collective-permute-start.7
  356.1 7.5 %collective-permute-start.8 = (bf16[1,128,512]{2,1,0:T(8,128)(2,1)S(1)}, bf16[1,128,512]{2,1,0:T(8,128)(2,1)S(1)}, u32[]{:S(2)}, u32[]{:S(2)}) collective-permute-start(bf16[1,128,512]{2,1,0:T(8,128)(2,1)S(1)} %get-tuple-element.62), channel_id=1, source_target_pairs={{1,0},{2,1},{3,2},{4,3},{5,4},{6,5},{7,6},{8,7},{9,8},{10,9},{11,1... | collective-permute-start | bytes 393224 | tf_op jit(solution)/shard_map/ppermute | solution.py:23
  364.4 1.8 collective-permute-done.8
  (176 shorter events, 54.1 us)
Async XLA Ops:
  0.0 352.5 %copy-start = (bf16[512,512]{1,0:T(8,128)(2,1)S(1)}, bf16[512,512]{1,0:T(8,128)(2,1)}, u32[]{:S(2)}) copy-start(bf16[512,512]{1,0:T(8,128)(2,1)} %param.14) | copy-start | bytes 1572868
  1.4 57.6 %collective-permute-start = (bf16[2,8,512]{2,1,0:T(8,128)(2,1)}, bf16[2,8,512]{2,1,0:T(8,128)(2,1)}, u32[]{:S(2)}, u32[]{:S(2)}) collective-permute-start(bf16[2,8,512]{2,1,0:T(8,128)(2,1)} %pad_maximum_fusion.6), channel_id=1, source_target_pairs={{0,32},{32,64},{64,96},{96,128},{128,160},{160,192},{192,224},{224... | collective-permute-start | bytes 49160 | tf_op jit(solution)/shard_map/ppermute | solution.py:12
  92.2 6.4 %collective-permute-start.1 = (bf16[2,8,512]{2,1,0:T(8,128)(2,1)}, bf16[2,8,512]{2,1,0:T(8,128)(2,1)S(1)}, u32[]{:S(2)}, u32[]{:S(2)}) collective-permute-start(bf16[2,8,512]{2,1,0:T(8,128)(2,1)} %collective-permute-done), channel_id=1, source_target_pairs={{0,32},{32,64},{64,96},{96,128},{128,160},{160,192},{192,224},{224... | collective-permute-start | bytes 49160 | tf_op jit(solution)/shard_map/ppermute | solution.py:12
  133.5 6.6 %collective-permute-start.2 = (bf16[2,8,512]{2,1,0:T(8,128)(2,1)}, bf16[2,8,512]{2,1,0:T(8,128)(2,1)S(1)}, u32[]{:S(2)}, u32[]{:S(2)}) collective-permute-start(bf16[2,8,512]{2,1,0:T(8,128)(2,1)} %copy-done.25), channel_id=1, source_target_pairs={{0,32},{32,64},{64,96},{96,128},{128,160},{160,192},{192,224},{224... | collective-permute-start | bytes 49160 | tf_op jit(solution)/shard_map/ppermute | solution.py:12
  173.6 7.0 %collective-permute-start.3 = (bf16[2,8,512]{2,1,0:T(8,128)(2,1)}, bf16[2,8,512]{2,1,0:T(8,128)(2,1)S(1)}, u32[]{:S(2)}, u32[]{:S(2)}) collective-permute-start(bf16[2,8,512]{2,1,0:T(8,128)(2,1)} %copy-done.26), channel_id=1, source_target_pairs={{0,32},{32,64},{64,96},{96,128},{128,160},{160,192},{192,224},{224... | collective-permute-start | bytes 49160 | tf_op jit(solution)/shard_map/ppermute | solution.py:12
  215.0 2.8 copy-start.24
  215.0 5.7 %copy-start.15 = (f32[8,256]{1,0:T(8,128)S(1)}, f32[8,256]{1,0:T(8,128)}, u32[]{:S(2)}) copy-start(f32[8,256]{1,0:T(8,128)} %get-tuple-element.77) | copy-start | bytes 24580
  215.0 5.7 %copy-start.17 = (f32[8,256]{1,0:T(8,128)S(1)}, f32[8,256]{1,0:T(8,128)}, u32[]{:S(2)}) copy-start(f32[8,256]{1,0:T(8,128)} %get-tuple-element.79) | copy-start | bytes 24580
  217.9 6.1 %copy-start.19 = (f32[8,256]{1,0:T(8,128)}, f32[8,256]{1,0:T(8,128)S(1)}, u32[]{:S(2)}) copy-start(f32[8,256]{1,0:T(8,128)S(1)} %get-tuple-element.75) | copy-start | bytes 24580
  217.9 6.1 %collective-permute-start.4 = (bf16[2,8,512]{2,1,0:T(8,128)(2,1)S(1)}, bf16[2,8,512]{2,1,0:T(8,128)(2,1)S(1)}, u32[]{:S(2)}, u32[]{:S(2)}) collective-permute-start(bf16[2,8,512]{2,1,0:T(8,128)(2,1)S(1)} %copy-done.24), channel_id=1, source_target_pairs={{0,32},{32,64},{64,96},{96,128},{128,160},{160,192},{192,224},{224... | collective-permute-start | bytes 49160 | tf_op jit(solution)/shard_map/ppermute | solution.py:12
  258.0 6.4 %collective-permute-start.5 = (bf16[2,8,512]{2,1,0:T(8,128)(2,1)}, bf16[2,8,512]{2,1,0:T(8,128)(2,1)S(1)}, u32[]{:S(2)}, u32[]{:S(2)}) collective-permute-start(bf16[2,8,512]{2,1,0:T(8,128)(2,1)} %copy-done.28), channel_id=1, source_target_pairs={{0,32},{32,64},{64,96},{96,128},{128,160},{160,192},{192,224},{224... | collective-permute-start | bytes 49160 | tf_op jit(solution)/shard_map/ppermute | solution.py:12
  298.9 7.1 %collective-permute-start.6 = (bf16[2,8,512]{2,1,0:T(8,128)(2,1)}, bf16[2,8,512]{2,1,0:T(8,128)(2,1)S(1)}, u32[]{:S(2)}, u32[]{:S(2)}) collective-permute-start(bf16[2,8,512]{2,1,0:T(8,128)(2,1)} %copy-done.27), channel_id=1, source_target_pairs={{0,32},{32,64},{64,96},{96,128},{128,160},{160,192},{192,224},{224... | collective-permute-start | bytes 49160 | tf_op jit(solution)/shard_map/ppermute | solution.py:12
  337.8 2.6 copy-start.16
  338.8 2.7 copy-start.1
  341.2 1.6 copy-start.2
  341.5 2.0 copy-start.3
  342.8 1.7 copy-start.4
  343.5 1.7 copy-start.5
  344.6 1.7 copy-start.6
  351.6 15.1 %slice-start = ((s8[4718592]{0:T(1024)(128)(4,1)}), s8[4194304]{0:T(1024)(128)(4,1)S(1)}, s32[]{:S(2)}) async-start(s8[4718592]{0:T(1024)(128)(4,1)} %bitcast.311), calls=%async_computation | async-start | bytes 8388608
  352.1 1.2 copy-start.14
  353.3 13.4 %slice-start.1 = ((s8[4718592]{0:T(1024)(128)(4,1)}), s8[524288]{0:T(1024)(128)(4,1)S(1)}, s32[]{:S(2)}) async-start(s8[4718592]{0:T(1024)(128)(4,1)} %bitcast.311), calls=%async_computation.1 | async-start | bytes 1048576
  353.9 10.5 %collective-permute-start.7 = (bf16[1,128,512]{2,1,0:T(8,128)(2,1)S(1)}, bf16[1,128,512]{2,1,0:T(8,128)(2,1)S(1)}, u32[]{:S(2)}, u32[]{:S(2)}) collective-permute-start(bf16[1,128,512]{2,1,0:T(8,128)(2,1)S(1)} %get-tuple-element.63), channel_id=1, source_target_pairs={{0,1},{1,2},{2,3},{3,4},{4,5},{5,6},{6,7},{7,8},{8,9},{9,10},{10,1... | collective-permute-start | bytes 393224 | tf_op jit(solution)/shard_map/ppermute | solution.py:20
  356.1 10.0 %collective-permute-start.8 = (bf16[1,128,512]{2,1,0:T(8,128)(2,1)S(1)}, bf16[1,128,512]{2,1,0:T(8,128)(2,1)S(1)}, u32[]{:S(2)}, u32[]{:S(2)}) collective-permute-start(bf16[1,128,512]{2,1,0:T(8,128)(2,1)S(1)} %get-tuple-element.62), channel_id=1, source_target_pairs={{1,0},{2,1},{3,2},{4,3},{5,4},{6,5},{7,6},{8,7},{9,8},{10,9},{11,1... | collective-permute-start | bytes 393224 | tf_op jit(solution)/shard_map/ppermute | solution.py:23
  (17 other events, 13.6 us)
where the time goes:
time: 376 us; the launch traced here: 370 us
  blocking collectives  266 us (71%)
  matrix products  35.6 us (9%)
  local copies, waits for them, and re-layouts  28 us (7%)
  starting transfers between devices  27.9 us (7%)
  other arithmetic  6.82 us (2%)
  waiting for transfers between devices  5.17 us (1%)
    all_gather x8, blocking collectives, visit_shards(): collected = lax.all_gather(block, 'tile', axis=1, tiled=True)  266 us
    dot_general x8, matrix products, attend(): jnp.einsum('qhd,khd->hqk', query_heads, keys, preferred_element_type=jnp....  21.3 us
    ppermute x7, starting transfers between devices, passed_along(): lax.ppermute(array, axis, [(i, (i + by) % peers) for i in range(peers)])  18.1 us
    unnamed x65, local copies, waits for them, and re-layouts  9.9 us
  transfers between devices with their start and end apart: 9, of which 4 were waited for; matrix products, arithmetic and copies ran while one was open for 10% of the time, Pallas kernels for 0%

commit v1 on v0

v1 whole, which is shorter than its diff:
```python
import jax
import jax.numpy as jnp
from jax import lax
from jax.experimental import pallas as pl
from jax.experimental.pallas import tpu as pltpu
from jax.sharding import PartitionSpec as P

MESH = pl.DeviceIdType.MESH
NX, NY, NZ = 4, 4, 8
LON = 128
D = 512
ROWS = 256
PAIRS = 4
NEG = -1e30
F32 = jnp.float32
BF16 = jnp.bfloat16


def ring(i, n):
    return lax.rem(i + n, n)


def device(x, y, z, core):
    return (x * 2 + y // 2, z * 4 + lax.rem(y, 2) * 2 + core)


def kernel(
    mask_ref, valid_ref, feat_hbm, q_hbm, k_hbm, v_hbm, wo_hbm, wc_hbm, out_ref,
    own, stage, kv, bias, q_ref, qe, feat, wo, wc, acc, top, mixed, nrm, halo,
    load_sem, z_send, z_recv, send_sem, near_recv, sib_recv, halo_send, halo_recv,
):
    blk = lax.axis_index("blk")
    tile = lax.axis_index("tile")
    x = blk // 2
    y = lax.rem(blk, 2) * 2 + lax.rem(tile // 2, 2)
    z = tile // 4
    core = lax.rem(tile, 2)
    sib = device(x, y, z, 1 - core)
    me = blk * 32 + tile
    nxt = lax.rem(me + 1, 256)
    prv = lax.rem(me + 255, 256)
    nxt_id = (nxt // 32, lax.rem(nxt, 32))
    prv_id = (prv // 32, lax.rem(prv, 32))
    side = 1 - 2 * core

    loads = [
        pltpu.make_async_copy(k_hbm, own.at[0], load_sem.at[0]),
        pltpu.make_async_copy(v_hbm, own.at[1], load_sem.at[1]),
        pltpu.make_async_copy(q_hbm, q_ref, load_sem.at[2]),
        pltpu.make_async_copy(feat_hbm, feat, load_sem.at[3]),
        pltpu.make_async_copy(wo_hbm, wo, load_sem.at[4]),
        pltpu.make_async_copy(wc_hbm, wc, load_sem.at[5]),
    ]
    loads[0].start()
    loads[1].start()

    barrier = pltpu.get_barrier_semaphore()

    def greet(dev):
        pl.semaphore_signal(barrier, inc=1, device_id=dev, device_id_type=MESH)

    greet(sib)
    for dz in range(1, NZ):
        for c in range(2):
            greet(device(x, y, ring(z + dz, NZ), c))
    for d in (1, 3):
        greet(device(ring(x + d, NX), y, z, core))
        greet(device(x, ring(y + d, NY), z, core))
    greet(nxt_id)
    greet(prv_id)
    for load in loads[2:]:
        load.start()
    loads[0].wait()
    loads[1].wait()
    pl.semaphore_wait(barrier, 21)

    def z_copy(dz, c):
        return pltpu.make_async_remote_copy(
            src_ref=own.at[c],
            dst_ref=stage.at[z, core],
            send_sem=z_send.at[dz, c],
            recv_sem=z_recv.at[z, core],
            device_id=device(x, y, ring(z + dz, NZ), c),
            device_id_type=MESH,
        )

    for dz in (4, 3, 5, 2, 6, 1, 7):
        for c in range(2):
            z_copy(dz, c).start()
    sib_copy = pltpu.make_async_remote_copy(
        src_ref=own.at[1 - core],
        dst_ref=stage.at[z, core],
        send_sem=z_send.at[0, 0],
        recv_sem=z_recv.at[z, core],
        device_id=sib,
        device_id_type=MESH,
    )
    sib_copy.start()
    stage[z, core] = own[core]

    loads[2].wait()
    lane = lax.broadcasted_iota(jnp.int32, (ROWS, 128), 1)
    row = lax.broadcasted_iota(jnp.int32, (ROWS, 128), 0)
    onehot = jnp.where(lane == row // LON, 1.0, 0.0).astype(BF16)
    for p in range(PAIRS):
        part = q_ref[:, p * 128 : (p + 1) * 128].astype(F32) * 0.125
        qe[p, :ROWS, :128] = jnp.where(lane < 64, part, 0.0).astype(BF16)
        qe[p, ROWS:, :128] = jnp.where(lane >= 64, part, 0.0).astype(BF16)
        qe[p, :ROWS, 128:] = onehot
        qe[p, ROWS:, 128:] = onehot

    key = lax.broadcasted_iota(jnp.int32, (128, 128), 0)
    col = lax.broadcasted_iota(jnp.int32, (128, 128), 1)
    low = key < 64

    def mask_block(i, carry):
        kx, ky = i // NY, lax.rem(i, NY)
        b0 = kx * 4 + (ky // 2) * 2
        b1 = b0 + 1
        place = ((key >> 4) & 3) * 32 + (key & 15) + lax.rem(ky, 2) * 16
        limit = jnp.where(low, valid_ref[b0], valid_ref[b1])
        first = jnp.where(low, mask_ref[0, b0], mask_ref[0, b1])
        second = jnp.where(low, mask_ref[1, b0], mask_ref[1, b1])
        wanted = jnp.where(col == 0, first, second)
        live = jnp.where(place < limit, wanted, 0)
        live = jnp.where(col < 2, live, 1)
        bias[kx, ky] = jnp.where(live > 0, 0.0, NEG).astype(BF16)
        return carry

    lax.fori_loop(0, NX * NY, mask_block, 0)

    for dz in range(NZ):
        for c in range(2):
            src_z = ring(z + dz, NZ)

            def arrival(cc):
                return pltpu.make_async_remote_copy(
                    src_ref=own.at[0],
                    dst_ref=stage.at[src_z, cc],
                    send_sem=z_send.at[0, 1],
                    recv_sem=z_recv.at[src_z, cc],
                    device_id=sib,
                    device_id_type=MESH,
                )

            if dz == 0:
                if c == 0:
                    arrival(1 - core).wait_recv()
            else:
                arrival(c).wait_recv()
    block = stage[...].astype(F32).reshape(128, D).astype(BF16)

    uv = ((x, y), (y, x))
    for half in range(2):
        u, v = uv[half]
        kv[core, half, u, v] = block[:, half * 256 : (half + 1) * 256]

    def dev_of(half, u, v, c):
        return device(u, v, z, c) if half == 0 else device(v, u, z, c)

    slots = {}

    def copy_block(half, bu, bv, name, target, recv):
        slot = slots.setdefault((half, name), len(slots))
        return pltpu.make_async_remote_copy(
            src_ref=kv.at[core, half, bu, bv],
            dst_ref=kv.at[core, half, bu, bv],
            send_sem=send_sem.at[slot],
            recv_sem=recv.at[half, bu, bv],
            device_id=target,
            device_id_type=MESH,
        )

    sent = []

    def send(half, bu, bv, name, target, recv=None):
        copy = copy_block(half, bu, bv, name, target, near_recv if recv is None else recv)
        copy.start()
        sent.append(copy)

    def wait_near(half, bu, bv):
        pltpu.make_async_remote_copy(
            src_ref=kv.at[core, half, bu, bv],
            dst_ref=kv.at[core, half, bu, bv],
            send_sem=send_sem.at[0],
            recv_sem=near_recv.at[half, bu, bv],
            device_id=sib,
            device_id_type=MESH,
        ).wait_recv()

    def wait_sib(half, bu, bv):
        pltpu.make_async_remote_copy(
            src_ref=kv.at[1 - core, half, bu, bv],
            dst_ref=kv.at[1 - core, half, bu, bv],
            send_sem=send_sem.at[0],
            recv_sem=sib_recv.at[half, bu, bv],
            device_id=sib,
            device_id_type=MESH,
        ).wait_recv()

    def spread(half, bv, tag):
        u, v = uv[half]
        for d in (1, 3):
            send(half, u, bv, ("u", tag, d), dev_of(half, ring(u + d, 4), v, core))
        send(half, u, bv, ("sib", tag), sib, sib_recv)

    for half in range(2):
        u, v = uv[half]
        for d in (1, 3):
            send(half, u, v, ("v", d), dev_of(half, u, ring(v + d, 4), core))
    for half in range(2):
        spread(half, uv[half][1], 0)
    for half in range(2):
        u, v = uv[half]
        back = ring(v - side, 4)
        wait_near(half, u, back)
        send(half, u, back, ("v", "relay"), dev_of(half, u, ring(v + side, 4), core))
        spread(half, back, 1)
    for half in range(2):
        u, v = uv[half]
        ahead = ring(v + side, 4)
        wait_near(half, u, ahead)
        spread(half, ahead, 2)
    for half in range(2):
        u, v = uv[half]
        far = ring(v + 2, 4)
        wait_near(half, u, far)
        spread(half, far, 3)

    ones = jnp.ones((512, 128), BF16)

    def attend(half, bu, first):
        def one_pair(p, carry):
            pair = half * 2 + p
            cols = pl.ds(pl.multiple_of(p * 128, 128), 128)
            keys = kv[0, half, bu, :, :, cols].reshape(512, 128)
            values = kv[1, half, bu, :, :, cols].reshape(512, 128)
            if half == 0:
                shut = bias[bu].reshape(512, 128)
            else:
                shut = bias[:, bu].reshape(512, 128)
            scores = lax.dot_general(
                qe[pair],
                jnp.concatenate([keys, shut], axis=1),
                (((1,), (1,)), ((), ())),
                preferred_element_type=F32,
            )
            peak = jnp.max(scores, axis=1, keepdims=True)
            if first:
                new_top = jnp.broadcast_to(peak, (512, 128))
            else:
                old_top = top[pair]
                new_top = jnp.maximum(old_top, peak)
            weights = jnp.exp(scores - jnp.concatenate([new_top] * 4, axis=1)).astype(BF16)
            part = jnp.dot(
                weights, jnp.concatenate([values, ones], axis=1), preferred_element_type=F32
            )
            if first:
                acc[pair] = part
            else:
                factor = jnp.exp(old_top - new_top)
                acc[pair] = acc[pair] * jnp.concatenate([factor] * 2, axis=1) + part
            top[pair] = new_top
            return carry

        lax.fori_loop(0, 2, one_pair, 0)

    order = [lambda w: w, lambda w: ring(w - side, 4), lambda w: ring(w + side, 4), lambda w: ring(w + 2, 4)]
    vorder = order

    for half in range(2):
        u, v = uv[half]
        for f in vorder:
            wait_sib(half, u, f(v))
        attend(half, u, True)

    for half in range(2):
        u, v = uv[half]
        bu = order[1](u)
        for i, f in enumerate(vorder):
            wait_near(half, bu, f(v))
            send(half, bu, f(v), ("relay", i), dev_of(half, ring(u + side, 4), v, core))
            send(half, bu, f(v), ("sib1", i), sib, sib_recv)
    for half in range(2):
        u, v = uv[half]
        bu = order[2](u)
        for i, f in enumerate(vorder):
            wait_near(half, bu, f(v))
            send(half, bu, f(v), ("sib2", i), sib, sib_recv)
    for step in (1, 2):
        for half in range(2):
            u, v = uv[half]
            bu = order[step](u)
            for f in vorder:
                wait_sib(half, bu, f(v))
            attend(half, bu, False)
    for half in range(2):
        u, v = uv[half]
        bu = order[3](u)
        for i, f in enumerate(vorder):
            wait_near(half, bu, f(v))
            send(half, bu, f(v), ("sib3", i), sib, sib_recv)
    for half in range(2):
        u, v = uv[half]
        bu = order[3](u)
        for f in vorder:
            wait_sib(half, bu, f(v))
        attend(half, bu, False)

    for pair in range(PAIRS):
        even = acc[pair, :ROWS, :128] / acc[pair, :ROWS, 128:]
        odd = acc[pair, ROWS:, :128] / acc[pair, ROWS:, 128:]
        mixed[:, pair * 128 : (pair + 1) * 128] = jnp.where(lane < 64, even, odd).astype(BF16)

    loads[3].wait()
    loads[4].wait()
    projected = jnp.dot(mixed[...], wo[...], preferred_element_type=F32)
    hidden = (feat[...].astype(F32) + projected).astype(BF16)
    wide = hidden.astype(F32)
    feat[...] = hidden
    normed = (wide * lax.rsqrt(jnp.mean(wide * wide, axis=-1, keepdims=True) + 1e-06)).astype(BF16)
    nrm[...] = normed.reshape(2, LON, D)

    up = pltpu.make_async_remote_copy(
        src_ref=nrm.at[0], dst_ref=halo.at[1], send_sem=halo_send.at[0],
        recv_sem=halo_recv.at[1], device_id=prv_id, device_id_type=MESH,
    )
    down = pltpu.make_async_remote_copy(
        src_ref=nrm.at[1], dst_ref=halo.at[0], send_sem=halo_send.at[1],
        recv_sem=halo_recv.at[0], device_id=nxt_id, device_id_type=MESH,
    )
    up.start()
    down.start()

    def neighbours(field):
        wide_field = field.astype(F32)
        left = pltpu.roll(wide_field, 1, 0).astype(BF16)
        right = pltpu.roll(wide_field, LON - 1, 0).astype(BF16)
        return jnp.concatenate([left, field, right], axis=1)

    loads[5].wait()
    both = jnp.concatenate([neighbours(nrm[0]), neighbours(nrm[1])], axis=1)
    top_row = jnp.dot(both, wc[1:3].reshape(6 * D, D), preferred_element_type=F32)
    low_row = jnp.dot(both, wc[0:2].reshape(6 * D, D), preferred_element_type=F32)

    down.wait_recv()
    above = jnp.where(me > 0, halo[0].astype(F32), 0.0).astype(BF16)
    top_row = top_row + jnp.dot(
        neighbours(above), wc[0].reshape(3 * D, D), preferred_element_type=F32
    )
    out_ref[:LON] = (feat[:LON].astype(F32) + top_row).astype(BF16)
    up.wait_recv()
    below = jnp.where(me < 255, halo[1].astype(F32), 0.0).astype(BF16)
    low_row = low_row + jnp.dot(
        neighbours(below), wc[2].reshape(3 * D, D), preferred_element_type=F32
    )
    out_ref[LON:] = (feat[LON:].astype(F32) + low_row).astype(BF16)

    for dz in range(1, NZ):
        for c in range(2):
            z_copy(dz, c).wait_send()
    sib_copy.wait_send()
    for copy in sent:
        copy.wait_send()
    up.wait_send()
    down.wait_send()


def on_device(grid_feat, queries, obs_keys, obs_values, block_mask, obs_valid, out_weight, conv_weight):
    hbm = pl.BlockSpec(memory_space=pl.ANY)
    smem = pl.BlockSpec(memory_space=pltpu.SMEM)
    return pl.pallas_call(
        kernel,
        out_shape=jax.ShapeDtypeStruct((ROWS, D), BF16),
        in_specs=[smem, smem] + [hbm] * 6,
        out_specs=pl.BlockSpec(memory_space=pltpu.VMEM),
        scratch_shapes=[
            pltpu.VMEM((2, 8, D), BF16),
            pltpu.VMEM((NZ, 2, 8, D), BF16),
            pltpu.VMEM((2, 2, 4, 4, 128, 256), BF16),
            pltpu.VMEM((NX, NY, 128, 128), BF16),
            pltpu.VMEM((ROWS, D), BF16),
            pltpu.VMEM((PAIRS, 512, 256), BF16),
            pltpu.VMEM((ROWS, D), BF16),
            pltpu.VMEM((D, D), BF16),
            pltpu.VMEM((3, 3, D, D), BF16),
            pltpu.VMEM((PAIRS, 512, 256), F32),
            pltpu.VMEM((PAIRS, 512, 128), F32),
            pltpu.VMEM((ROWS, D), BF16),
            pltpu.VMEM((2, LON, D), BF16),
            pltpu.VMEM((2, LON, D), BF16),
            pltpu.SemaphoreType.DMA((6,)),
            pltpu.SemaphoreType.DMA((NZ, 2)),
            pltpu.SemaphoreType.DMA((NZ, 2)),
            pltpu.SemaphoreType.DMA((64,)),
            pltpu.SemaphoreType.DMA((2, 4, 4)),
            pltpu.SemaphoreType.DMA((2, 4, 4)),
            pltpu.SemaphoreType.DMA((2,)),
            pltpu.SemaphoreType.DMA((2,)),
        ],
        compiler_params=pltpu.CompilerParams(
            collective_id=0, has_side_effects=True, vmem_limit_bytes=48 * 1024 * 1024
        ),
    )(block_mask, obs_valid, grid_feat, queries, obs_keys, obs_values, out_weight, conv_weight)


def solution(mesh):
    rows = P(("blk", "tile"), None)
    return jax.shard_map(
        on_device,
        mesh=mesh,
        in_specs=(rows, rows, rows, rows, rows, P(), P(), P()),
        out_specs=rows,
        check_vma=False,
    )
```

time: 376 us -> 58.3 us (0.16); the launches traced: 370 us -> 58 us
  blocking collectives: 266 us -> 0 us
  Pallas kernels: 0 us -> 49.2 us
  matrix products: 35.6 us -> 0 us
  starting transfers between devices: 27.9 us -> 0 us
  local copies, waits for them, and re-layouts: 28 us -> 8.71 us
  other arithmetic: 6.82 us -> 0 us
  waiting for transfers between devices: 5.17 us -> 0 us
    all_gather x8 -> x0, blocking collectives: 266 us -> none  [visit_shards(): collected = lax.all_gather(block, 'tile', axis=1, tiled=True)]
    pallas_call x0 -> x1, Pallas kernels: none -> 49.2 us  [on_device(): pl.pallas_call(kernel, out_shape=jax.ShapeDtypeStruct((ROWS, D), BF16), i...]
    dot_general x34 -> x0, matrix products: 35.6 us -> none  [the longest x8 21.3 us: attend(): jnp.einsum('qhd,khd->hqk', query_heads, keys, preferred_element_type=jnp....]
    ppermute x9 -> x0, starting transfers between devices: 27.9 us -> none  [the longest x7 18.1 us: passed_along(): lax.ppermute(array, axis, [(i, (i + by) % peers) for i in range(peers)])]
    slice x26 -> x0, local copies, waits for them, and re-layouts: 12.4 us -> none  [the longest x15 6.26 us: attend(): values = kv_rows[1].reshape(rows, HEADS, head)]
    broadcast_in_dim x16 -> x0, local copies, waits for them, and re-layouts: 5.78 us -> none  [attend(): jnp.where(allowed[None, :, None, :], scores, -jnp.inf)]
    ppermute x9 -> x0, waiting for transfers between devices: 5.17 us -> none  [the longest x7 2.69 us: passed_along(): lax.ppermute(array, axis, [(i, (i + by) % peers) for i in range(peers)])]
    unnamed x65 -> x17, local copies, waits for them, and re-layouts: 9.9 us -> 8.71 us
  transfers between devices with their start and end apart: 9 -> 0, of which waited for: 4 -> 0; matrix products, arithmetic and copies ran while one was open for 10% -> 0% of each run, Pallas kernels for 0% -> 0%
where the time goes in v1:
time: 58.3 us; the launch traced here: 58 us
  Pallas kernels  49.2 us (84%)
  local copies, waits for them, and re-layouts  8.71 us (15%)
    pallas_call x1, Pallas kernels, on_device(): pl.pallas_call(kernel, out_shape=jax.ShapeDtypeStruct((ROWS, D), BF16), i...  49.2 us
    unnamed x17, local copies, waits for them, and re-layouts  8.71 us

profile of v1, /device:TPU:2, one launch (start us, length us, event | category | flops | bytes accessed | tf_op | source)
XLA Modules:
  0.0 58.0 jit_solution(4806375330422177763)
XLA Ops:
  0.0 0.0 copy-start
  0.0 2.3 %copy-done = bf16[3,3,512,512]{3,2,1,0:T(8,128)(2,1)S(1)} copy-done((bf16[3,3,512,512]{3,2,1,0:T(8,128)(2,1)S(1)}, bf16[3,3,512,512]{3,2,1,0:T(8,128)(2,1)}, u32[]{:S(2)}) %copy-start) | copy-done | bytes 4718616
  2.3 0.0 copy-start.1
  2.3 1.0 %copy-done.1 = bf16[512,512]{1,0:T(8,128)(2,1)S(1)} copy-done((bf16[512,512]{1,0:T(8,128)(2,1)S(1)}, bf16[512,512]{1,0:T(8,128)(2,1)}, u32[]{:S(2)}) %copy-start.1) | copy-done | bytes 524312
  3.4 0.0 copy-start.2
  3.4 0.9 %copy-done.2 = bf16[256,512]{1,0:T(8,128)(2,1)S(1)} copy-done((bf16[256,512]{1,0:T(8,128)(2,1)S(1)}, bf16[256,512]{1,0:T(8,128)(2,1)}, u32[]{:S(2)}) %copy-start.2) | copy-done | bytes 262168
  4.3 0.0 copy-start.3
  4.3 0.9 %copy-done.3 = bf16[256,512]{1,0:T(8,128)(2,1)S(1)} copy-done((bf16[256,512]{1,0:T(8,128)(2,1)S(1)}, bf16[256,512]{1,0:T(8,128)(2,1)}, u32[]{:S(2)}) %copy-start.3) | copy-done | bytes 262168
  5.3 0.0 copy-start.4
  5.3 0.7 %copy-done.4 = bf16[8,512]{1,0:T(8,128)(2,1)S(1)} copy-done((bf16[8,512]{1,0:T(8,128)(2,1)S(1)}, bf16[8,512]{1,0:T(8,128)(2,1)}, u32[]{:S(2)}) %copy-start.4) | copy-done | bytes 8216
  6.0 0.0 copy-start.5
  6.0 0.7 %copy-done.5 = bf16[8,512]{1,0:T(8,128)(2,1)S(1)} copy-done((bf16[8,512]{1,0:T(8,128)(2,1)S(1)}, bf16[8,512]{1,0:T(8,128)(2,1)}, u32[]{:S(2)}) %copy-start.5) | copy-done | bytes 8216
  6.7 0.0 copy-start.6
  6.7 0.7 %copy-done.6 = s32[2,16]{1,0:T(2,128)S(1)} copy-done((s32[2,16]{1,0:T(2,128)S(1)}, s32[2,16]{1,0:T(2,128)}, u32[]{:S(2)}) %copy-start.6) | copy-done | bytes 152
  7.4 0.0 copy-start.7
  7.4 0.7 %copy-done.7 = s32[16]{0:T(128)S(1)} copy-done((s32[16]{0:T(128)S(1)}, s32[16]{0:T(128)}, u32[]{:S(2)}) %copy-start.7) | copy-done | bytes 88
  8.0 49.2 %shard_map.82 = bf16[256,512]{1,0:T(8,128)(2,1)S(1)} custom-call(s32[2,16]{1,0:T(2,128)S(1)} %copy-done.6, s32[16]{0:T(128)S(1)} %copy-done.7, bf16[256,512]{1,0:T(8,128)(2,1)S(1)} %copy-done.2, bf16[256,512]{1,0:T(8,128)(2,1)S(1)} %copy-done.3, bf16[8,512]{1,0:T(8,128)(2,1)S(1)} %copy-done.4, bf16[8,512]{1,0:T(8,128)(2,1)S(1)} %copy-done.5, ...), custom_call_target="tpu_custom_call" | custom-call | tf_op jit(solution)/shard_map/pallas_call | solution.py:372
  57.3 0.7 %copy.10 = bf16[256,512]{1,0:T(8,128)(2,1)} copy(bf16[256,512]{1,0:T(8,128)(2,1)S(1)} %shard_map.82) | data formatting | bytes 524288
Async XLA Ops:
  0.0 2.3 %copy-start = (bf16[3,3,512,512]{3,2,1,0:T(8,128)(2,1)S(1)}, bf16[3,3,512,512]{3,2,1,0:T(8,128)(2,1)}, u32[]{:S(2)}) copy-start(bf16[3,3,512,512]{3,2,1,0:T(8,128)(2,1)} %wc_hbm.1) | copy-start | bytes 14155780
  2.3 1.0 %copy-start.1 = (bf16[512,512]{1,0:T(8,128)(2,1)S(1)}, bf16[512,512]{1,0:T(8,128)(2,1)}, u32[]{:S(2)}) copy-start(bf16[512,512]{1,0:T(8,128)(2,1)} %wo_hbm.1) | copy-start | bytes 1572868
  3.4 0.9 %copy-start.2 = (bf16[256,512]{1,0:T(8,128)(2,1)S(1)}, bf16[256,512]{1,0:T(8,128)(2,1)}, u32[]{:S(2)}) copy-start(bf16[256,512]{1,0:T(8,128)(2,1)} %feat_hbm.1) | copy-start | bytes 786436
  4.3 0.9 %copy-start.3 = (bf16[256,512]{1,0:T(8,128)(2,1)S(1)}, bf16[256,512]{1,0:T(8,128)(2,1)}, u32[]{:S(2)}) copy-start(bf16[256,512]{1,0:T(8,128)(2,1)} %q_hbm.1) | copy-start | bytes 786436
  5.3 0.7 %copy-start.4 = (bf16[8,512]{1,0:T(8,128)(2,1)S(1)}, bf16[8,512]{1,0:T(8,128)(2,1)}, u32[]{:S(2)}) copy-start(bf16[8,512]{1,0:T(8,128)(2,1)} %k_hbm.1) | copy-start | bytes 24580
  6.0 0.7 %copy-start.5 = (bf16[8,512]{1,0:T(8,128)(2,1)S(1)}, bf16[8,512]{1,0:T(8,128)(2,1)}, u32[]{:S(2)}) copy-start(bf16[8,512]{1,0:T(8,128)(2,1)} %v_hbm.1) | copy-start | bytes 24580
  6.7 0.7 %copy-start.6 = (s32[2,16]{1,0:T(2,128)S(1)}, s32[2,16]{1,0:T(2,128)}, u32[]{:S(2)}) copy-start(s32[2,16]{1,0:T(2,128)} %mask_ref.1) | copy-start | bytes 388
  7.4 0.7 %copy-start.7 = (s32[16]{0:T(128)S(1)}, s32[16]{0:T(128)}, u32[]{:S(2)}) copy-start(s32[16]{0:T(128)} %valid_ref.1) | copy-start | bytes 196

commit v2 on v1

--- a/solution.py
+++ b/solution.py
@@ -25,8 +25,8 @@
 
 
 def kernel(
-    mask_ref, valid_ref, feat_hbm, q_hbm, k_hbm, v_hbm, wo_hbm, wc_hbm, out_ref,
-    own, stage, kv, bias, q_ref, qe, feat, wo, wc, acc, top, mixed, nrm, halo,
+    mask_hbm, valid_hbm, feat_hbm, q_hbm, k_hbm, v_hbm, wo_hbm, wc_hbm, out_ref,
+    mask_ref, valid_ref, own, stage, kv, bias, q_ref, qe, feat, wo, wc, acc, top, mixed, nrm, halo,
     load_sem, z_send, z_recv, send_sem, near_recv, sib_recv, halo_send, halo_recv,
 ):
     blk = lax.axis_index("blk")
@@ -50,6 +50,8 @@
         pltpu.make_async_copy(feat_hbm, feat, load_sem.at[3]),
         pltpu.make_async_copy(wo_hbm, wo, load_sem.at[4]),
         pltpu.make_async_copy(wc_hbm, wc, load_sem.at[5]),
+        pltpu.make_async_copy(mask_hbm, mask_ref, load_sem.at[6]),
+        pltpu.make_async_copy(valid_hbm, valid_ref, load_sem.at[7]),
     ]
     loads[0].start()
     loads[1].start()
@@ -112,6 +114,9 @@
     key = lax.broadcasted_iota(jnp.int32, (128, 128), 0)
     col = lax.broadcasted_iota(jnp.int32, (128, 128), 1)
     low = key < 64
+
+    loads[6].wait()
+    loads[7].wait()
 
     def mask_block(i, carry):
         kx, ky = i // NY, lax.rem(i, NY)
@@ -367,14 +372,15 @@
 
 
 def on_device(grid_feat, queries, obs_keys, obs_values, block_mask, obs_valid, out_weight, conv_weight):
-    hbm = pl.BlockSpec(memory_space=pl.ANY)
-    smem = pl.BlockSpec(memory_space=pltpu.SMEM)
+    hbm = pl.BlockSpec(memory_space=pltpu.HBM)
     return pl.pallas_call(
         kernel,
         out_shape=jax.ShapeDtypeStruct((ROWS, D), BF16),
-        in_specs=[smem, smem] + [hbm] * 6,
+        in_specs=[hbm] * 8,
         out_specs=pl.BlockSpec(memory_space=pltpu.VMEM),
         scratch_shapes=[
+            pltpu.SMEM((2, 16), jnp.int32),
+            pltpu.SMEM((16,), jnp.int32),
             pltpu.VMEM((2, 8, D), BF16),
             pltpu.VMEM((NZ, 2, 8, D), BF16),
             pltpu.VMEM((2, 2, 4, 4, 128, 256), BF16),
@@ -389,7 +395,7 @@
             pltpu.VMEM((ROWS, D), BF16),
             pltpu.VMEM((2, LON, D), BF16),
             pltpu.VMEM((2, LON, D), BF16),
-            pltpu.SemaphoreType.DMA((6,)),
+            pltpu.SemaphoreType.DMA((8,)),
             pltpu.SemaphoreType.DMA((NZ, 2)),
             pltpu.SemaphoreType.DMA((NZ, 2)),
             pltpu.SemaphoreType.DMA((64,)),
@@ -399,7 +405,7 @@
             pltpu.SemaphoreType.DMA((2,)),
         ],
         compiler_params=pltpu.CompilerParams(
-            collective_id=0, has_side_effects=True, vmem_limit_bytes=48 * 1024 * 1024
+            collective_id=0, has_side_effects=True, vmem_limit_bytes=58 * 1024 * 1024
         ),
     )(block_mask, obs_valid, grid_feat, queries, obs_keys, obs_values, out_weight, conv_weight)
 

time: 58.3 us -> 51 us (0.87)
  local copies, waits for them, and re-layouts: 8.71 us -> 1.67 us
    unnamed x17 -> x1, local copies, waits for them, and re-layouts: 8.71 us -> 1.67 us
where the time goes in v2:
time: 51 us; the launch traced here: 50.9 us
  Pallas kernels  49.2 us (96%)
  local copies, waits for them, and re-layouts  1.67 us (3%)
    pallas_call x1, Pallas kernels, on_device(): pl.pallas_call(kernel, out_shape=jax.ShapeDtypeStruct((ROWS, D), BF16), i...  49.2 us
    unnamed x1, local copies, waits for them, and re-layouts  1.67 us

profile of v2, /device:TPU:2, one launch (start us, length us, event | category | flops | bytes accessed | tf_op | source)
XLA Modules:
  0.0 50.9 jit_solution(15011069036270398846)
XLA Ops:
  0.0 49.2 %shard_map.82 = bf16[256,512]{1,0:T(8,128)(2,1)} custom-call(s32[2,16]{1,0:T(2,128)} %mask_hbm.1, s32[16]{0:T(128)} %valid_hbm.1, bf16[256,512]{1,0:T(8,128)(2,1)} %feat_hbm.1, bf16[256,512]{1,0:T(8,128)(2,1)} %q_hbm.1, bf16[8,512]{1,0:T(8,128)(2,1)} %k_hbm.1, bf16[8,512]{1,0:T(8,128)(2,1)} %v_hbm.1, bf16[512,512]{1,0:T(8,128)(2,1)} %wo_hbm.1, ...), custom_call_target="tpu_custom_call" | custom-call | tf_op jit(solution)/shard_map/pallas_call | solution.py:376
  49.2 1.7 %copy.10 = bf16[256,512]{1,0:T(8,128)(2,1)} copy(bf16[256,512]{1,0:T(8,128)(2,1)} %shard_map.82) | data formatting | bytes 524288

commit v3 on v2

--- a/solution.py
+++ b/solution.py
@@ -26,7 +26,7 @@
 
 def kernel(
     mask_hbm, valid_hbm, feat_hbm, q_hbm, k_hbm, v_hbm, wo_hbm, wc_hbm, out_ref,
-    mask_ref, valid_ref, own, stage, kv, bias, q_ref, qe, feat, wo, wc, acc, top, mixed, nrm, halo,
+    mask_ref, valid_ref, own, stage, kv, bias, q_ref, qt, feat, wo, wc, acc, top, mixed, nrm, halo,
     load_sem, z_send, z_recv, send_sem, near_recv, sib_recv, halo_send, halo_recv,
 ):
     blk = lax.axis_index("blk")
@@ -101,15 +101,15 @@
     stage[z, core] = own[core]
 
     loads[2].wait()
-    lane = lax.broadcasted_iota(jnp.int32, (ROWS, 128), 1)
-    row = lax.broadcasted_iota(jnp.int32, (ROWS, 128), 0)
-    onehot = jnp.where(lane == row // LON, 1.0, 0.0).astype(BF16)
+    feat_row = lax.broadcasted_iota(jnp.int32, (128, ROWS), 0)
+    query_col = lax.broadcasted_iota(jnp.int32, (128, ROWS), 1)
+    onehot = jnp.where(feat_row == query_col // LON, 1.0, 0.0).astype(BF16)
     for p in range(PAIRS):
-        part = q_ref[:, p * 128 : (p + 1) * 128].astype(F32) * 0.125
-        qe[p, :ROWS, :128] = jnp.where(lane < 64, part, 0.0).astype(BF16)
-        qe[p, ROWS:, :128] = jnp.where(lane >= 64, part, 0.0).astype(BF16)
-        qe[p, :ROWS, 128:] = onehot
-        qe[p, ROWS:, 128:] = onehot
+        part = (q_ref[:, p * 128 : (p + 1) * 128].astype(F32) * 0.125).T
+        qt[p, :128, :ROWS] = jnp.where(feat_row < 64, part, 0.0).astype(BF16)
+        qt[p, :128, ROWS:] = jnp.where(feat_row >= 64, part, 0.0).astype(BF16)
+        qt[p, 128:, :ROWS] = onehot
+        qt[p, 128:, ROWS:] = onehot
 
     key = lax.broadcasted_iota(jnp.int32, (128, 128), 0)
     col = lax.broadcasted_iota(jnp.int32, (128, 128), 1)
@@ -153,7 +153,9 @@
                     arrival(1 - core).wait_recv()
             else:
                 arrival(c).wait_recv()
-    block = stage[...].astype(F32).reshape(128, D).astype(BF16)
+    plain = stage[...].astype(F32).reshape(128, D)
+    turned = jnp.concatenate([plain[:, p * 128 : (p + 1) * 128].T for p in range(PAIRS)], axis=1)
+    block = jnp.where(core == 0, plain, turned).astype(BF16)
 
     uv = ((x, y), (y, x))
     for half in range(2):
@@ -209,113 +211,125 @@
             send(half, u, bv, ("u", tag, d), dev_of(half, ring(u + d, 4), v, core))
         send(half, u, bv, ("sib", tag), sib, sib_recv)
 
-    for half in range(2):
-        u, v = uv[half]
-        for d in (1, 3):
-            send(half, u, v, ("v", d), dev_of(half, u, ring(v + d, 4), core))
-    for half in range(2):
-        spread(half, uv[half][1], 0)
-    for half in range(2):
-        u, v = uv[half]
-        back = ring(v - side, 4)
-        wait_near(half, u, back)
-        send(half, u, back, ("v", "relay"), dev_of(half, u, ring(v + side, 4), core))
-        spread(half, back, 1)
-    for half in range(2):
-        u, v = uv[half]
-        ahead = ring(v + side, 4)
-        wait_near(half, u, ahead)
-        spread(half, ahead, 2)
-    for half in range(2):
-        u, v = uv[half]
-        far = ring(v + 2, 4)
-        wait_near(half, u, far)
-        spread(half, far, 3)
-
-    ones = jnp.ones((512, 128), BF16)
-
-    def attend(half, bu, first):
-        def one_pair(p, carry):
+    ones = jnp.ones((16, 512), BF16)
+
+    def attend(half, blocks, first):
+        for p in range(2):
             pair = half * 2 + p
-            cols = pl.ds(pl.multiple_of(p * 128, 128), 128)
-            keys = kv[0, half, bu, :, :, cols].reshape(512, 128)
-            values = kv[1, half, bu, :, :, cols].reshape(512, 128)
-            if half == 0:
-                shut = bias[bu].reshape(512, 128)
-            else:
-                shut = bias[:, bu].reshape(512, 128)
-            scores = lax.dot_general(
-                qe[pair],
-                jnp.concatenate([keys, shut], axis=1),
-                (((1,), (1,)), ((), ())),
+            cols = slice(p * 128, (p + 1) * 128)
+            keys = [kv[0, half, bu, bv, :, cols] for bu, bv in blocks]
+            values = [kv[1, half, bu, bv, :, cols] for bu, bv in blocks]
+            shut = [bias[bu, bv] if half == 0 else bias[bv, bu] for bu, bv in blocks]
+            scores = jnp.dot(
+                jnp.concatenate(
+                    [jnp.concatenate(keys, axis=0), jnp.concatenate(shut, axis=0)], axis=1
+                ),
+                qt[pair],
                 preferred_element_type=F32,
             )
-            peak = jnp.max(scores, axis=1, keepdims=True)
+            peak = jnp.max(scores, axis=0, keepdims=True)
             if first:
-                new_top = jnp.broadcast_to(peak, (512, 128))
+                new_top = jnp.broadcast_to(peak, (8, 512))
             else:
                 old_top = top[pair]
                 new_top = jnp.maximum(old_top, peak)
-            weights = jnp.exp(scores - jnp.concatenate([new_top] * 4, axis=1)).astype(BF16)
+            weights = jnp.exp(scores - new_top[:1]).astype(BF16)
             part = jnp.dot(
-                weights, jnp.concatenate([values, ones], axis=1), preferred_element_type=F32
+                jnp.concatenate([jnp.concatenate(values, axis=1), ones], axis=0),
+                weights,
+                preferred_element_type=F32,
             )
             if first:
                 acc[pair] = part
             else:
                 factor = jnp.exp(old_top - new_top)
-                acc[pair] = acc[pair] * jnp.concatenate([factor] * 2, axis=1) + part
+                acc[pair] = acc[pair] * factor[:1] + part
             top[pair] = new_top
-            return carry
-
-        lax.fori_loop(0, 2, one_pair, 0)
-
-    order = [lambda w: w, lambda w: ring(w - side, 4), lambda w: ring(w + side, 4), lambda w: ring(w + 2, 4)]
-    vorder = order
-
+
+    us = []
+    vs = []
     for half in range(2):
         u, v = uv[half]
-        for f in vorder:
-            wait_sib(half, u, f(v))
-        attend(half, u, True)
-
-    for half in range(2):
+        us.append((u, ring(u - side, 4), ring(u + side, 4), ring(u + 2, 4)))
+        vs.append((v, ring(v - side, 4), ring(v + side, 4), ring(v + 2, 4)))
+    OWN, BACK, AHEAD, FAR = 0, 1, 2, 3
+
+    def both(step, *args):
+        for half in range(2):
+            step(half, *args)
+
+    def line_sends(half):
         u, v = uv[half]
-        bu = order[1](u)
-        for i, f in enumerate(vorder):
-            wait_near(half, bu, f(v))
-            send(half, bu, f(v), ("relay", i), dev_of(half, ring(u + side, 4), v, core))
-            send(half, bu, f(v), ("sib1", i), sib, sib_recv)
-    for half in range(2):
+        for d in (1, 3):
+            send(half, u, v, ("v", d), dev_of(half, u, ring(v + d, 4), core))
+
+    def line_block(half, c):
         u, v = uv[half]
-        bu = order[2](u)
-        for i, f in enumerate(vorder):
-            wait_near(half, bu, f(v))
-            send(half, bu, f(v), ("sib2", i), sib, sib_recv)
-    for step in (1, 2):
-        for half in range(2):
-            u, v = uv[half]
-            bu = order[step](u)
-            for f in vorder:
-                wait_sib(half, bu, f(v))
-            attend(half, bu, False)
-    for half in range(2):
-        u, v = uv[half]
-        bu = order[3](u)
-        for i, f in enumerate(vorder):
-            wait_near(half, bu, f(v))
-            send(half, bu, f(v), ("sib3", i), sib, sib_recv)
-    for half in range(2):
-        u, v = uv[half]
-        bu = order[3](u)
-        for f in vorder:
-            wait_sib(half, bu, f(v))
-        attend(half, bu, False)
+        bv = vs[half][c]
+        if c != OWN:
+            wait_near(half, u, bv)
+        if c == BACK:
+            send(half, u, bv, ("v", "relay"), dev_of(half, u, vs[half][AHEAD], core))
+        spread(half, bv, c)
+
+    def from_back(half, c):
+        bu, bv = us[half][BACK], vs[half][c]
+        wait_near(half, bu, bv)
+        send(half, bu, bv, ("relay", c), dev_of(half, us[half][AHEAD], uv[half][1], core))
+        send(half, bu, bv, ("sib1", c), sib, sib_recv)
+
+    def from_ahead(half, c):
+        bu, bv = us[half][AHEAD], vs[half][c]
+        wait_near(half, bu, bv)
+        send(half, bu, bv, ("sib2", c), sib, sib_recv)
+
+    def from_far(half, c):
+        bu, bv = us[half][FAR], vs[half][c]
+        wait_near(half, bu, bv)
+        send(half, bu, bv, ("sib3", c), sib, sib_recv)
+
+    def chunk(half, places, first=False):
+        blocks = [(us[half][a], vs[half][b]) for a, b in places]
+        for bu, bv in blocks:
+            wait_sib(half, bu, bv)
+        attend(half, blocks, first)
+
+    line = [(OWN, c) for c in (OWN, BACK, AHEAD, FAR)]
+    close = [(a, c) for a in (BACK, AHEAD) for c in (OWN, BACK)]
+    wide_off = [(a, c) for a in (BACK, AHEAD) for c in (AHEAD, FAR)]
+    last = [(FAR, c) for c in (OWN, BACK, AHEAD, FAR)]
+
+    both(line_sends)
+    both(line_block, OWN)
+    both(line_block, BACK)
+    both(line_block, AHEAD)
+    both(from_back, OWN)
+    both(from_ahead, OWN)
+    both(line_block, FAR)
+    chunk(0, line, True)
+    both(from_back, BACK)
+    both(from_ahead, BACK)
+    chunk(1, line, True)
+    both(from_back, AHEAD)
+    both(from_ahead, AHEAD)
+    both(from_far, OWN)
+    both(from_back, FAR)
+    both(from_ahead, FAR)
+    both(from_far, BACK)
+    chunk(0, close)
+    chunk(1, close)
+    both(from_far, AHEAD)
+    chunk(0, wide_off)
+    chunk(1, wide_off)
+    both(from_far, FAR)
+    chunk(0, last)
+    chunk(1, last)
 
     for pair in range(PAIRS):
-        even = acc[pair, :ROWS, :128] / acc[pair, :ROWS, 128:]
-        odd = acc[pair, ROWS:, :128] / acc[pair, ROWS:, 128:]
-        mixed[:, pair * 128 : (pair + 1) * 128] = jnp.where(lane < 64, even, odd).astype(BF16)
+        share = 1.0 / acc[pair, 128:129, :]
+        even = acc[pair, :64, :ROWS] * share[:, :ROWS]
+        odd = acc[pair, 64:128, ROWS:] * share[:, ROWS:]
+        mixed[:, pair * 128 : (pair + 1) * 128] = jnp.concatenate([even, odd], axis=0).T.astype(BF16)
 
     loads[3].wait()
     loads[4].wait()
@@ -344,9 +358,9 @@
         return jnp.concatenate([left, field, right], axis=1)
 
     loads[5].wait()
-    both = jnp.concatenate([neighbours(nrm[0]), neighbours(nrm[1])], axis=1)
-    top_row = jnp.dot(both, wc[1:3].reshape(6 * D, D), preferred_element_type=F32)
-    low_row = jnp.dot(both, wc[0:2].reshape(6 * D, D), preferred_element_type=F32)
+    pair_rows = jnp.concatenate([neighbours(nrm[0]), neighbours(nrm[1])], axis=1)
+    top_row = jnp.dot(pair_rows, wc[1:3].reshape(6 * D, D), preferred_element_type=F32)
+    low_row = jnp.dot(pair_rows, wc[0:2].reshape(6 * D, D), preferred_element_type=F32)
 
     down.wait_recv()
     above = jnp.where(me > 0, halo[0].astype(F32), 0.0).astype(BF16)
@@ -386,12 +400,12 @@
             pltpu.VMEM((2, 2, 4, 4, 128, 256), BF16),
             pltpu.VMEM((NX, NY, 128, 128), BF16),
             pltpu.VMEM((ROWS, D), BF16),
-            pltpu.VMEM((PAIRS, 512, 256), BF16),
+            pltpu.VMEM((PAIRS, 256, 512), BF16),
             pltpu.VMEM((ROWS, D), BF16),
             pltpu.VMEM((D, D), BF16),
             pltpu.VMEM((3, 3, D, D), BF16),
-            pltpu.VMEM((PAIRS, 512, 256), F32),
-            pltpu.VMEM((PAIRS, 512, 128), F32),
+            pltpu.VMEM((PAIRS, 144, 512), F32),
+            pltpu.VMEM((PAIRS, 8, 512), F32),
             pltpu.VMEM((ROWS, D), BF16),
             pltpu.VMEM((2, LON, D), BF16),
             pltpu.VMEM((2, LON, D), BF16),

time: 51 us -> 48 us (0.941)
  Pallas kernels: 49.2 us -> 46.2 us
    pallas_call x1, Pallas kernels: 49.2 us -> 46.2 us  [on_device(): pl.pallas_call(kernel, out_shape=jax.ShapeDtypeStruct((ROWS, D), BF16), i...]
where the time goes in v3:
time: 48 us; the launch traced here: 47.9 us
  Pallas kernels  46.2 us (96%)
  local copies, waits for them, and re-layouts  1.67 us (3%)
    pallas_call x1, Pallas kernels, on_device(): pl.pallas_call(kernel, out_shape=jax.ShapeDtypeStruct((ROWS, D), BF16), i...  46.2 us
    unnamed x1, local copies, waits for them, and re-layouts  1.67 us

profile of v3, /device:TPU:2, one launch (start us, length us, event | category | flops | bytes accessed | tf_op | source)
XLA Modules:
  0.0 47.9 jit_solution(3818600752756066699)
XLA Ops:
  0.0 46.2 %shard_map.82 = bf16[256,512]{1,0:T(8,128)(2,1)} custom-call(s32[2,16]{1,0:T(2,128)} %mask_hbm.1, s32[16]{0:T(128)} %valid_hbm.1, bf16[256,512]{1,0:T(8,128)(2,1)} %feat_hbm.1, bf16[256,512]{1,0:T(8,128)(2,1)} %q_hbm.1, bf16[8,512]{1,0:T(8,128)(2,1)} %k_hbm.1, bf16[8,512]{1,0:T(8,128)(2,1)} %v_hbm.1, bf16[512,512]{1,0:T(8,128)(2,1)} %wo_hbm.1, ...), custom_call_target="tpu_custom_call" | custom-call | tf_op jit(solution)/shard_map/pallas_call | solution.py:390
  46.2 1.7 %copy.10 = bf16[256,512]{1,0:T(8,128)(2,1)} copy(bf16[256,512]{1,0:T(8,128)(2,1)} %shard_map.82) | data formatting | bytes 524288

commit v4 on v3

--- a/solution.py
+++ b/solution.py
@@ -65,7 +65,7 @@
     for dz in range(1, NZ):
         for c in range(2):
             greet(device(x, y, ring(z + dz, NZ), c))
-    for d in (1, 3):
+    for d in (1, 2, 3):
         greet(device(ring(x + d, NX), y, z, core))
         greet(device(x, ring(y + d, NY), z, core))
     greet(nxt_id)
@@ -74,7 +74,7 @@
         load.start()
     loads[0].wait()
     loads[1].wait()
-    pl.semaphore_wait(barrier, 21)
+    pl.semaphore_wait(barrier, 23)
 
     def z_copy(dz, c):
         return pltpu.make_async_remote_copy(
@@ -251,8 +251,9 @@
     for half in range(2):
         u, v = uv[half]
         us.append((u, ring(u - side, 4), ring(u + side, 4), ring(u + 2, 4)))
-        vs.append((v, ring(v - side, 4), ring(v + side, 4), ring(v + 2, 4)))
-    OWN, BACK, AHEAD, FAR = 0, 1, 2, 3
+        vs.append((v, ring(v + 1, 4), ring(v - 1, 4), ring(v + 2, 4)))
+    OWN, NEXT, PREV, FAR = 0, 1, 2, 3
+    BACK, AHEAD = 1, 2
 
     def both(step, *args):
         for half in range(2):
@@ -260,17 +261,19 @@
 
     def line_sends(half):
         u, v = uv[half]
-        for d in (1, 3):
+        for d in (1, 3, 2):
             send(half, u, v, ("v", d), dev_of(half, u, ring(v + d, 4), core))
 
-    def line_block(half, c):
+    def line_near(half):
         u, v = uv[half]
-        bv = vs[half][c]
-        if c != OWN:
-            wait_near(half, u, bv)
-        if c == BACK:
-            send(half, u, bv, ("v", "relay"), dev_of(half, u, vs[half][AHEAD], core))
-        spread(half, bv, c)
+        wait_near(half, u, vs[half][NEXT])
+        spread(half, vs[half][NEXT], NEXT)
+        wait_near(half, u, vs[half][PREV])
+        spread(half, vs[half][PREV], PREV)
+
+    def line_far(half):
+        wait_near(half, uv[half][0], vs[half][FAR])
+        spread(half, vs[half][FAR], FAR)
 
     def from_back(half, c):
         bu, bv = us[half][BACK], vs[half][c]
@@ -294,34 +297,34 @@
             wait_sib(half, bu, bv)
         attend(half, blocks, first)
 
-    line = [(OWN, c) for c in (OWN, BACK, AHEAD, FAR)]
-    close = [(a, c) for a in (BACK, AHEAD) for c in (OWN, BACK)]
-    wide_off = [(a, c) for a in (BACK, AHEAD) for c in (AHEAD, FAR)]
-    last = [(FAR, c) for c in (OWN, BACK, AHEAD, FAR)]
+    line = [(OWN, c) for c in (OWN, NEXT, PREV, FAR)]
+    close = [(a, c) for a in (BACK, AHEAD) for c in (OWN, NEXT)]
+    wide_off = [(a, c) for a in (BACK, AHEAD) for c in (PREV, FAR)]
+    last = [(FAR, c) for c in (OWN, NEXT, PREV, FAR)]
 
     both(line_sends)
-    both(line_block, OWN)
-    both(line_block, BACK)
-    both(line_block, AHEAD)
+    for half in range(2):
+        spread(half, uv[half][1], OWN)
+    both(line_near)
     both(from_back, OWN)
     both(from_ahead, OWN)
-    both(line_block, FAR)
+    both(line_far)
     chunk(0, line, True)
-    both(from_back, BACK)
-    both(from_ahead, BACK)
+    both(from_back, NEXT)
+    both(from_ahead, NEXT)
     chunk(1, line, True)
-    both(from_back, AHEAD)
-    both(from_ahead, AHEAD)
+    both(from_back, PREV)
+    both(from_ahead, PREV)
     both(from_far, OWN)
+    chunk(0, close)
     both(from_back, FAR)
+    both(from_far, NEXT)
+    chunk(1, close)
     both(from_ahead, FAR)
-    both(from_far, BACK)
-    chunk(0, close)
-    chunk(1, close)
-    both(from_far, AHEAD)
+    both(from_far, PREV)
     chunk(0, wide_off)
+    both(from_far, FAR)
     chunk(1, wide_off)
-    both(from_far, FAR)
     chunk(0, last)
     chunk(1, last)
 

time: 48 us -> 46.3 us (0.965)
  Pallas kernels: 46.2 us -> 44.5 us
    pallas_call x1, Pallas kernels: 46.2 us -> 44.5 us  [on_device(): pl.pallas_call(kernel, out_shape=jax.ShapeDtypeStruct((ROWS, D), BF16), i...]
where the time goes in v4:
time: 46.3 us; the launch traced here: 46.1 us
  Pallas kernels  44.5 us (96%)
  local copies, waits for them, and re-layouts  1.67 us (4%)
    pallas_call x1, Pallas kernels, on_device(): pl.pallas_call(kernel, out_shape=jax.ShapeDtypeStruct((ROWS, D), BF16), i...  44.5 us
    unnamed x1, local copies, waits for them, and re-layouts  1.67 us

profile of v4, /device:TPU:2, one launch (start us, length us, event | category | flops | bytes accessed | tf_op | source)
XLA Modules:
  0.0 46.1 jit_solution(16042220655767050712)
XLA Ops:
  0.0 44.5 %shard_map.82 = bf16[256,512]{1,0:T(8,128)(2,1)} custom-call(s32[2,16]{1,0:T(2,128)} %mask_hbm.1, s32[16]{0:T(128)} %valid_hbm.1, bf16[256,512]{1,0:T(8,128)(2,1)} %feat_hbm.1, bf16[256,512]{1,0:T(8,128)(2,1)} %q_hbm.1, bf16[8,512]{1,0:T(8,128)(2,1)} %k_hbm.1, bf16[8,512]{1,0:T(8,128)(2,1)} %v_hbm.1, bf16[512,512]{1,0:T(8,128)(2,1)} %wo_hbm.1, ...), custom_call_target="tpu_custom_call" | custom-call | tf_op jit(solution)/shard_map/pallas_call | solution.py:393
  44.5 1.7 %copy.10 = bf16[256,512]{1,0:T(8,128)(2,1)} copy(bf16[256,512]{1,0:T(8,128)(2,1)} %shard_map.82) | data formatting | bytes 524288

commit v5 on v4

--- a/solution.py
+++ b/solution.py
@@ -211,9 +211,9 @@
             send(half, u, bv, ("u", tag, d), dev_of(half, ring(u + d, 4), v, core))
         send(half, u, bv, ("sib", tag), sib, sib_recv)
 
-    ones = jnp.ones((16, 512), BF16)
 
     def attend(half, blocks, first):
+        ones = jnp.ones((16, 128 * len(blocks)), BF16)
         for p in range(2):
             pair = half * 2 + p
             cols = slice(p * 128, (p + 1) * 128)
@@ -300,7 +300,8 @@
     line = [(OWN, c) for c in (OWN, NEXT, PREV, FAR)]
     close = [(a, c) for a in (BACK, AHEAD) for c in (OWN, NEXT)]
     wide_off = [(a, c) for a in (BACK, AHEAD) for c in (PREV, FAR)]
-    last = [(FAR, c) for c in (OWN, NEXT, PREV, FAR)]
+    early = [(FAR, c) for c in (OWN, NEXT)]
+    last = [(FAR, c) for c in (PREV, FAR)]
 
     both(line_sends)
     for half in range(2):
@@ -318,13 +319,15 @@
     both(from_far, OWN)
     chunk(0, close)
     both(from_back, FAR)
+    both(from_ahead, FAR)
+    chunk(1, close)
     both(from_far, NEXT)
-    chunk(1, close)
-    both(from_ahead, FAR)
+    chunk(0, wide_off)
+    chunk(1, wide_off)
     both(from_far, PREV)
-    chunk(0, wide_off)
     both(from_far, FAR)
-    chunk(1, wide_off)
+    chunk(0, early)
+    chunk(1, early)
     chunk(0, last)
     chunk(1, last)
 

time: 46.3 us -> 45.6 us (0.985)
  Pallas kernels: 44.5 us -> 43.8 us
    pallas_call x1, Pallas kernels: 44.5 us -> 43.8 us  [on_device(): pl.pallas_call(kernel, out_shape=jax.ShapeDtypeStruct((ROWS, D), BF16), i...]
where the time goes in v5:
time: 45.6 us; the launch traced here: 45.5 us
  Pallas kernels  43.8 us (96%)
  local copies, waits for them, and re-layouts  1.67 us (4%)
    pallas_call x1, Pallas kernels, on_device(): pl.pallas_call(kernel, out_shape=jax.ShapeDtypeStruct((ROWS, D), BF16), i...  43.8 us
    unnamed x1, local copies, waits for them, and re-layouts  1.67 us

profile of v5, /device:TPU:2, one launch (start us, length us, event | category | flops | bytes accessed | tf_op | source)
XLA Modules:
  0.0 45.5 jit_solution(14053555907485954237)
XLA Ops:
  0.0 43.8 %shard_map.82 = bf16[256,512]{1,0:T(8,128)(2,1)} custom-call(s32[2,16]{1,0:T(2,128)} %mask_hbm.1, s32[16]{0:T(128)} %valid_hbm.1, bf16[256,512]{1,0:T(8,128)(2,1)} %feat_hbm.1, bf16[256,512]{1,0:T(8,128)(2,1)} %q_hbm.1, bf16[8,512]{1,0:T(8,128)(2,1)} %k_hbm.1, bf16[8,512]{1,0:T(8,128)(2,1)} %v_hbm.1, bf16[512,512]{1,0:T(8,128)(2,1)} %wo_hbm.1, ...), custom_call_target="tpu_custom_call" | custom-call | tf_op jit(solution)/shard_map/pallas_call | solution.py:396
  43.8 1.7 %copy.10 = bf16[256,512]{1,0:T(8,128)(2,1)} copy(bf16[256,512]{1,0:T(8,128)(2,1)} %shard_map.82) | data formatting | bytes 524288

commit v6 on v5

--- a/solution.py
+++ b/solution.py
@@ -25,9 +25,9 @@
 
 
 def kernel(
-    mask_hbm, valid_hbm, feat_hbm, q_hbm, k_hbm, v_hbm, wo_hbm, wc_hbm, out_ref,
+    mask_hbm, valid_hbm, feat_hbm, q_hbm, k_hbm, v_hbm, wo_hbm, wc_hbm, out_hbm,
     mask_ref, valid_ref, own, stage, kv, bias, q_ref, qt, feat, wo, wc, acc, top, mixed, nrm, halo,
-    load_sem, z_send, z_recv, send_sem, near_recv, sib_recv, halo_send, halo_recv,
+    load_sem, z_send, z_recv, send_sem, near_recv, sib_recv, halo_send, halo_recv, out_ref, out_sem,
 ):
     blk = lax.axis_index("blk")
     tile = lax.axis_index("tile")
@@ -261,7 +261,7 @@
 
     def line_sends(half):
         u, v = uv[half]
-        for d in (1, 3, 2):
+        for d in (1, 3):
             send(half, u, v, ("v", d), dev_of(half, u, ring(v + d, 4), core))
 
     def line_near(half):
@@ -306,6 +306,9 @@
     both(line_sends)
     for half in range(2):
         spread(half, uv[half][1], OWN)
+    for half in range(2):
+        u, v = uv[half]
+        send(half, u, v, ("v", 2), dev_of(half, u, ring(v + 2, 4), core))
     both(line_near)
     both(from_back, OWN)
     both(from_ahead, OWN)
@@ -374,12 +377,16 @@
         neighbours(above), wc[0].reshape(3 * D, D), preferred_element_type=F32
     )
     out_ref[:LON] = (feat[:LON].astype(F32) + top_row).astype(BF16)
+    upper = pltpu.make_async_copy(out_ref.at[:LON], out_hbm.at[:LON], out_sem.at[0])
+    upper.start()
     up.wait_recv()
     below = jnp.where(me < 255, halo[1].astype(F32), 0.0).astype(BF16)
     low_row = low_row + jnp.dot(
         neighbours(below), wc[2].reshape(3 * D, D), preferred_element_type=F32
     )
     out_ref[LON:] = (feat[LON:].astype(F32) + low_row).astype(BF16)
+    lower = pltpu.make_async_copy(out_ref.at[LON:], out_hbm.at[LON:], out_sem.at[1])
+    lower.start()
 
     for dz in range(1, NZ):
         for c in range(2):
@@ -389,6 +396,8 @@
         copy.wait_send()
     up.wait_send()
     down.wait_send()
+    upper.wait()
+    lower.wait()
 
 
 def on_device(grid_feat, queries, obs_keys, obs_values, block_mask, obs_valid, out_weight, conv_weight):
@@ -397,7 +406,7 @@
         kernel,
         out_shape=jax.ShapeDtypeStruct((ROWS, D), BF16),
         in_specs=[hbm] * 8,
-        out_specs=pl.BlockSpec(memory_space=pltpu.VMEM),
+        out_specs=hbm,
         scratch_shapes=[
             pltpu.SMEM((2, 16), jnp.int32),
             pltpu.SMEM((16,), jnp.int32),
@@ -423,6 +432,8 @@
             pltpu.SemaphoreType.DMA((2, 4, 4)),
             pltpu.SemaphoreType.DMA((2,)),
             pltpu.SemaphoreType.DMA((2,)),
+            pltpu.VMEM((ROWS, D), BF16),
+            pltpu.SemaphoreType.DMA((2,)),
         ],
         compiler_params=pltpu.CompilerParams(
             collective_id=0, has_side_effects=True, vmem_limit_bytes=58 * 1024 * 1024

time: 45.6 us -> 45.2 us (level)
  no operation moved by 1% of the time
where the time goes in v6:
time: 45.2 us; the launch traced here: 45.1 us
  Pallas kernels  43.4 us (96%)
  local copies, waits for them, and re-layouts  1.67 us (4%)
    pallas_call x1, Pallas kernels, on_device(): pl.pallas_call(kernel, out_shape=jax.ShapeDtypeStruct((ROWS, D), BF16), i...  43.4 us
    unnamed x1, local copies, waits for them, and re-layouts  1.67 us

profile of v6, /device:TPU:2, one launch (start us, length us, event | category | flops | bytes accessed | tf_op | source)
XLA Modules:
  0.0 45.1 jit_solution(3715091670555312984)
XLA Ops:
  0.0 43.4 %shard_map.82 = bf16[256,512]{1,0:T(8,128)(2,1)} custom-call(s32[2,16]{1,0:T(2,128)} %mask_hbm.1, s32[16]{0:T(128)} %valid_hbm.1, bf16[256,512]{1,0:T(8,128)(2,1)} %feat_hbm.1, bf16[256,512]{1,0:T(8,128)(2,1)} %q_hbm.1, bf16[8,512]{1,0:T(8,128)(2,1)} %k_hbm.1, bf16[8,512]{1,0:T(8,128)(2,1)} %v_hbm.1, bf16[512,512]{1,0:T(8,128)(2,1)} %wo_hbm.1, ...), custom_call_target="tpu_custom_call" | custom-call | tf_op jit(solution)/shard_map/pallas_call | solution.py:405
  43.5 1.7 %copy.10 = bf16[256,512]{1,0:T(8,128)(2,1)} copy(bf16[256,512]{1,0:T(8,128)(2,1)} %shard_map.82) | data formatting | bytes 524288

commit v7 on v6

--- a/solution.py
+++ b/solution.py
@@ -342,13 +342,6 @@
 
     loads[3].wait()
     loads[4].wait()
-    projected = jnp.dot(mixed[...], wo[...], preferred_element_type=F32)
-    hidden = (feat[...].astype(F32) + projected).astype(BF16)
-    wide = hidden.astype(F32)
-    feat[...] = hidden
-    normed = (wide * lax.rsqrt(jnp.mean(wide * wide, axis=-1, keepdims=True) + 1e-06)).astype(BF16)
-    nrm[...] = normed.reshape(2, LON, D)
-
     up = pltpu.make_async_remote_copy(
         src_ref=nrm.at[0], dst_ref=halo.at[1], send_sem=halo_send.at[0],
         recv_sem=halo_recv.at[1], device_id=prv_id, device_id_type=MESH,
@@ -357,8 +350,15 @@
         src_ref=nrm.at[1], dst_ref=halo.at[0], send_sem=halo_send.at[1],
         recv_sem=halo_recv.at[0], device_id=nxt_id, device_id_type=MESH,
     )
-    up.start()
-    down.start()
+    for row_at, copy in ((1, down), (0, up)):
+        rows = slice(row_at * LON, (row_at + 1) * LON)
+        projected = jnp.dot(mixed[rows], wo[...], preferred_element_type=F32)
+        hidden = (feat[rows].astype(F32) + projected).astype(BF16)
+        wide = hidden.astype(F32)
+        feat[rows] = hidden
+        scale = lax.rsqrt(jnp.mean(wide * wide, axis=-1, keepdims=True) + 1e-06)
+        nrm[row_at] = (wide * scale).astype(BF16)
+        copy.start()
 
     def neighbours(field):
         wide_field = field.astype(F32)

time: 45.2 us -> 45.1 us (level)
  no operation moved by 1% of the time
where the time goes in v7:
time: 45.1 us; the launch traced here: 45 us
  Pallas kernels  43.3 us (96%)
  local copies, waits for them, and re-layouts  1.67 us (4%)
    pallas_call x1, Pallas kernels, on_device(): pl.pallas_call(kernel, out_shape=jax.ShapeDtypeStruct((ROWS, D), BF16), i...  43.3 us
    unnamed x1, local copies, waits for them, and re-layouts  1.67 us

profile of v7, /device:TPU:2, one launch (start us, length us, event | category | flops | bytes accessed | tf_op | source)
XLA Modules:
  0.0 45.0 jit_solution(9376672271004968579)
XLA Ops:
  0.0 43.3 %shard_map.82 = bf16[256,512]{1,0:T(8,128)(2,1)} custom-call(s32[2,16]{1,0:T(2,128)} %mask_hbm.1, s32[16]{0:T(128)} %valid_hbm.1, bf16[256,512]{1,0:T(8,128)(2,1)} %feat_hbm.1, bf16[256,512]{1,0:T(8,128)(2,1)} %q_hbm.1, bf16[8,512]{1,0:T(8,128)(2,1)} %k_hbm.1, bf16[8,512]{1,0:T(8,128)(2,1)} %v_hbm.1, bf16[512,512]{1,0:T(8,128)(2,1)} %wo_hbm.1, ...), custom_call_target="tpu_custom_call" | custom-call | tf_op jit(solution)/shard_map/pallas_call | solution.py:405
  43.4 1.7 %copy.10 = bf16[256,512]{1,0:T(8,128)(2,1)} copy(bf16[256,512]{1,0:T(8,128)(2,1)} %shard_map.82) | data formatting | bytes 524288
